TPU v7x, 32 devices: a whole 2x2x4 slice. The times are simulated.
32 devices in a mesh: groups: 2 (over x), expert: 16 (over z, y, core).
Axes of the slice: x: 2, y: 2, z: 4, core: 2. Of those that a mesh axis runs over, the one named last changes fastest.
Arguments:
- tokens: bfloat16 [256, 6144], P(('groups', 'expert')), parts along dimension 0, may hold values from -6 to 6
- norm_gain: float32 [6144], replicated, may hold values from 0.5 to 1.5
- router: bfloat16 [6144, 4], replicated, may hold values from -0.078125 to 0.078125
- w_gate: bfloat16 [6144, 4096], P(None, 'expert'), may hold values from -0.078125 to 0.078125
- w_up: bfloat16 [6144, 4096], P(None, 'expert'), may hold values from -0.078125 to 0.078125
- w_down: bfloat16 [4096, 6144], P('expert'), may hold values from -0.1875 to 0.1875
- expert_ids: int32 [256, 2], P(('groups', 'expert')), parts along dimension 0, may hold values from 0 to 3, as said below
- live_rows: int32 [32], P(('groups', 'expert')), parts along dimension 0, may hold values from 6 to 8, as said below
Outputs:
- mixed_out: bfloat16 [256, 6144], P(('groups', 'expert')), parts along dimension 0
There are 2 independent parts, one for each index of `groups`. A program takes and returns all parts, laid end to end along the dimension named above; an argument that names none is the same for every part. Nothing has to cross between parts.
Inputs may be any that keep to these rules, and one draw needn't show every extreme that they name: `expert_ids`: each row names two different experts. Among the live rows of one device no expert is named by more than 6 rows; in every draw some expert is named by exactly 6 live rows of every device. `live_rows`: rows at or beyond this count in a device's block are padding; some device is full in every draw.
All inputs are finite; a program needn't handle non-finite values.
Results may differ from a plain program's by a relative error of at most 0.0042.
Values may be sent and summed in bfloat16 or wider, within the bound.
A program may use at most 128 MiB of HBM per device.

v0:
```python
import jax
import jax.numpy as jnp
from jax import lax
from jax.sharding import PartitionSpec as P

CAP = 6


epsilon = 1e-05


def expert_ffn(received, w_gate, w_up, w_down):
    count_src, count_slot, model_width = received.shape
    flat_rows = received.reshape(count_src * count_slot, model_width)
    gate_proj = jnp.dot(flat_rows, w_gate, preferred_element_type=jnp.float32)
    up_proj = jnp.dot(flat_rows, w_up, preferred_element_type=jnp.float32)
    hidden = (jax.nn.silu(gate_proj) * up_proj).astype(jnp.bfloat16)
    partial_value = jnp.dot(hidden, w_down, preferred_element_type=jnp.float32).astype(jnp.bfloat16)
    return partial_value.reshape(count_src, count_slot, model_width)


def local(tokens, norm_gain, router, w_gate, w_up, w_down, expert_ids, live_rows):
    devices = lax.axis_size("expert")
    experts = router.shape[1]
    members = devices // experts
    row_count, model_width = tokens.shape
    capacity = CAP
    tok_f32 = tokens.astype(jnp.float32)
    scale_inv = lax.rsqrt(jnp.mean(tok_f32 * tok_f32, axis=-1, keepdims=True) + epsilon)
    normed = (tok_f32 * scale_inv * norm_gain).astype(jnp.bfloat16)
    logits = jnp.dot(normed, router, preferred_element_type=jnp.float32)
    expert_range = jnp.arange(experts, dtype=jnp.int32)
    one_hot = (expert_ids[:, :, None] == expert_range[None, None, :]).astype(jnp.float32)
    chosen = jnp.sum(one_hot * logits[:, None, :], axis=-1)
    gate_probs = jax.nn.sigmoid(chosen - chosen[:, ::-1])
    alive_mask = (jnp.arange(row_count, dtype=jnp.int32) < live_rows[0]).astype(jnp.float32)
    picked = one_hot * alive_mask[:, None, None]
    flat_pick = picked.reshape(row_count * 2, experts)
    earlier = jnp.cumsum(flat_pick, axis=0) - flat_pick
    slot_of = jnp.sum(earlier * flat_pick, axis=-1).reshape(row_count, 2)
    slot_range = jnp.arange(capacity, dtype=jnp.float32)
    placed = picked[:, :, :, None] * (
        slot_of[:, :, None, None] == slot_range[None, None, None, :]
    ).astype(jnp.float32)
    scatter_table = jnp.sum(placed, axis=1).reshape(row_count, experts * capacity)
    combine_table = jnp.sum(placed * gate_probs[:, :, None, None], axis=1).reshape(
        row_count, experts * capacity
    )
    buffer = jnp.dot(
        scatter_table.T.astype(jnp.bfloat16), normed, preferred_element_type=jnp.float32
    ).astype(jnp.bfloat16)
    outgoing = jnp.repeat(buffer.reshape(experts, capacity, model_width), members, axis=0)
    partials = expert_ffn(
        lax.all_to_all(outgoing, "expert", split_axis=0, concat_axis=0, tiled=True),
        w_gate,
        w_up,
        w_down,
    )
    returned = lax.all_to_all(partials, "expert", split_axis=0, concat_axis=0, tiled=True)
    group_sums = jnp.sum(
        returned.astype(jnp.float32).reshape(experts, members, capacity, model_width), axis=1
    )
    routed_out = jnp.dot(
        combine_table,
        group_sums.reshape(experts * capacity, model_width),
        precision=lax.Precision.HIGHEST,
        preferred_element_type=jnp.float32,
    )
    return (tok_f32 + routed_out).astype(jnp.bfloat16)


def solution(mesh):
    return jax.shard_map(
        local,
        mesh=mesh,
        in_specs=(
            P(("groups", "expert"), None),
            P(),
            P(),
            P(None, "expert"),
            P(None, "expert"),
            P("expert", None),
            P(("groups", "expert"), None),
            P(("groups", "expert")),
        ),
        out_specs=P(("groups", "expert"), None),
        check_vma=False,
    )
```

profile of v0, /device:TPU:0, one launch (start us, length us, event | category | flops | bytes accessed | tf_op | source)
XLA Modules:
  0.0 108.3 jit_solution(8735853380296695285)
XLA Ops:
  0.0 0.0 copy-start
  0.8 1.2 %fusion.4 = f32[8]{0:T(128)S(1)} fusion(bf16[8,6144]{1,0:T(8,128)(2,1)} %param.8), kind=kLoop, calls=%fused_computation.11 | loop fusion | flops 147448 | bytes 98336 | tf_op jit(solution)/shard_map/reduce_sum | solution.py:29
  2.0 0.8 copy.15
  2.8 1.1 %fusion.15 = f32[8,4]{0,1:T(4,128)S(1)} fusion(bf16[6144,4]{0,1:T(4,128)(2,1)} %param.10, bf16[8,6144]{1,0:T(8,128)(2,1)} %param.8, f32[6144]{0:T(1024)} %param.9, f32[8]{0:T(128)S(1)} %add_rsqrt_fusion), kind=kOutput, calls=%fused_computation.23 | convolution fusion | flops 589824 | bytes 172192 | tf_op jit(solution)/shard_map/dot_general | solution.py:31
  3.9 0.7 select_reduce_fusion
  4.7 0.1 mul.77
  4.7 0.1 mul.78
  4.8 0.1 eq.49
  4.9 0.1 fusion.18
  5.0 0.2 fusion.17
  5.2 0.1 eq.53
  5.3 0.1 copy.16
  5.4 0.1 copy.17
  5.6 0.1 convert_element_type.47
  5.6 1.9 %convolution_convert_fusion.1 = bf16[24,6144]{1,0:T(8,128)(2,1)} fusion(bf16[8,24]{1,0:T(8,128)(2,1)S(1)} %convert_element_type.47, bf16[8,6144]{1,0:T(8,128)(2,1)} %param.8, f32[6144]{0:T(1024)} %param.9, f32[8]{0:T(128)S(1)} %add_rsqrt_fusion), kind=kOutput, calls=%fused_computation.1 | convolution fusion | flops 2703360 | bytes 418208 | tf_op jit(solution)/shard_map/dot_general | solution.py:49
  7.6 1.1 reshape.56
  8.6 0.1 broadcast_in_dim.2
  8.8 43.2 %all_to_all.10 = bf16[16,6,6144]{2,1,0:T(8,128)(2,1)} all-to-all(bf16[16,6,6144]{2,1,0:T(8,128)(2,1)S(1)} %bitcast.20), channel_id=1, replica_groups=mesh['groups'=2,'expert'=16] {'expert'}, dimensions={0} | all-to-all | bytes 2359296 | tf_op jit(solution)/shard_map/all_to_all | solution.py:54
  52.0 2.4 %reshape.58 = bf16[96,6144]{1,0:T(8,128)(2,1)} reshape(bf16[16,6,6144]{2,1,0:T(8,128)(2,1)} %all_to_all.10) | data formatting | bytes 2359296 | tf_op jit(solution)/shard_map/reshape | solution.py:14
  54.4 2.9 %fusion.22 = f32[96,256]{1,0:T(8,128)S(1)} fusion(bf16[96,6144]{1,0:T(8,128)(2,1)} %reshape.58, bf16[6144,256]{1,0:T(8,128)(2,1)} %param.11), kind=kOutput, calls=%fused_computation.37 | convolution fusion | flops 301989888 | bytes 4423680 | tf_op jit(solution)/shard_map/dot_general | solution.py:15
  57.3 0.0 copy-done
  57.3 5.1 %convolution_convert_fusion = bf16[96,6144]{1,0:T(8,128)(2,1)} fusion(bf16[256,6144]{1,0:T(8,128)(2,1)S(1)} %copy-done, bf16[96,6144]{1,0:T(8,128)(2,1)} %reshape.58, bf16[6144,256]{1,0:T(8,128)(2,1)} %param.12, f32[96,256]{1,0:T(8,128)S(1)} %fusion.22), kind=kOutput, calls=%fused_computation | convolution fusion | flops 604717056 | bytes 8749056 | tf_op jit(solution)/shard_map/dot_general | solution.py:18
  62.5 2.4 %reshape.59 = bf16[16,6,6144]{2,1,0:T(8,128)(2,1)} reshape(bf16[96,6144]{1,0:T(8,128)(2,1)} %convolution_convert_fusion) | data formatting | bytes 2359296 | tf_op jit(solution)/shard_map/reshape | solution.py:19
  64.9 0.0 copy-start.1
  64.9 41.1 %all_to_all.11 = bf16[16,6,6144]{2,1,0:T(8,128)(2,1)S(1)} all-to-all(bf16[16,6,6144]{2,1,0:T(8,128)(2,1)} %reshape.59), channel_id=1, replica_groups=mesh['groups'=2,'expert'=16] {'expert'}, dimensions={0} | all-to-all | bytes 2359296 | tf_op jit(solution)/shard_map/all_to_all | solution.py:59
  106.0 0.4 convert_reduce_fusion
  106.4 0.0 copy-done.1
  106.4 1.9 %fusion.1 = bf16[8,6144]{1,0:T(8,128)(2,1)} fusion(f32[8,4,6]{0,1,2:T(4,128)S(1)} %get-tuple-element.6, f32[4,6,6144]{2,1,0:T(8,128)S(1)} %convert_reduce_fusion, bf16[8,6144]{1,0:T(8,128)(2,1)S(1)} %copy-done.1), kind=kOutput, calls=%fused_computation.4 | convolution fusion | flops 14303232 | bytes 787200 | tf_op jit(solution)/shard_map/dot_general | solution.py:63
  (7 shorter events, 0.1 us)
Async XLA Ops:
  0.0 57.3 %copy-start = (bf16[256,6144]{1,0:T(8,128)(2,1)S(1)}, bf16[256,6144]{1,0:T(8,128)(2,1)}, u32[]{:S(2)}) copy-start(bf16[256,6144]{1,0:T(8,128)(2,1)} %param.13) | copy-start | bytes 9437188
  64.9 41.5 %copy-start.1 = (bf16[8,6144]{1,0:T(8,128)(2,1)S(1)}, bf16[8,6144]{1,0:T(8,128)(2,1)}, u32[]{:S(2)}) copy-start(bf16[8,6144]{1,0:T(8,128)(2,1)} %param.8) | copy-start | bytes 294916
where the time goes:
time: 109 us; the launch traced here: 108 us
  blocking collectives  84.3 us (77%)
  matrix products  13 us (12%)
  local copies, waits for them, and re-layouts  7.44 us (7%)
  other arithmetic  2.66 us (2%)
    all_to_all x1, blocking collectives, local(): lax.all_to_all(outgoing, 'expert', split_axis=0, concat_axis=0, tiled=True)  43.2 us
    all_to_all x1, blocking collectives, local(): lax.all_to_all(partials, 'expert', split_axis=0, concat_axis=0, tiled=True)  41.1 us
    dot_general x1, matrix products, expert_ffn(): jnp.dot(hidden, w_down, preferred_element_type=jnp.float32)  5.15 us
    dot_general x1, matrix products, expert_ffn(): gate_proj = jnp.dot(flat_rows, w_gate, preferred_element_type=jnp.float32)  2.88 us
    reshape x1, local copies, waits for them, and re-layouts, expert_ffn(): return partial_value.reshape(count_src, count_slot, model_width)  2.43 us
    reshape x1, local copies, waits for them, and re-layouts, expert_ffn(): flat_rows = received.reshape(count_src * count_slot, model_width)  2.4 us

commit v1 on v0

v1 whole, which is shorter than its diff:
```python
import functools

import jax
import jax.numpy as jnp
from jax import lax
from jax.experimental import pallas as pl
from jax.experimental.pallas import tpu as pltpu
from jax.sharding import PartitionSpec as P

EPS = 1e-05
LANES = 128
GATHER_CHUNKS = 4
REDUCE_CHUNKS = 4
ROW_BLOCK = 128
CORES = 2


def _mod(a, n):
    return lax.rem(a + n, n)


def kernel(
    E, Q, B, D, H,
    live_ref, tok_hbm, gain_ref, router_ref, ids_ref, wg_hbm, wu_hbm, wd_hbm,
    out_ref,
    tok_ref, G, wg, wu, wd, acc_g, acc_u, hid, part, core_in, chip_sum, quad_in, plane, plane_in,
    load_sem, az_send, az_recv, aq_send, aq_recv, ac_send, ac_recv,
    rc_send, rc_recv, rq_send, rq_recv, rz_send, rz_recv,
):
    me = lax.axis_index("expert")
    members = Q * CORES
    e = me // members
    m = lax.rem(me, members)
    q = m // CORES
    c = lax.rem(m, CORES)
    rows = CORES * Q * E * B
    half = Q * E * B
    quad = E * B

    def dev(e_, q_, c_):
        return {"expert": (e_ * Q + q_) * CORES + c_}

    def slot(e_, q_, c_):
        return (c_ * Q + q_) * E + e_

    def remote(src, dst, ssem, rsem, device):
        return pltpu.make_async_remote_copy(
            src_ref=src, dst_ref=dst, send_sem=ssem, recv_sem=rsem,
            device_id=device, device_id_type=pl.DeviceIdType.MESH,
        )

    def wait_bytes(ref, sem):
        pltpu.make_async_copy(ref, ref, sem).wait()

    barrier = pltpu.get_barrier_semaphore()
    others_e = [_mod(e + d, E) for d in range(1, E)]
    others_q = [_mod(q + d, Q) for d in range(1, Q)]
    for e2 in others_e:
        pl.semaphore_signal(barrier, inc=1, device_id=dev(e2, q, c), device_id_type=pl.DeviceIdType.MESH)
    for q2 in others_q:
        pl.semaphore_signal(barrier, inc=1, device_id=dev(e, q2, c), device_id_type=pl.DeviceIdType.MESH)
    pl.semaphore_signal(barrier, inc=1, device_id=dev(e, q, 1 - c), device_id_type=pl.DeviceIdType.MESH)

    tok_load = pltpu.make_async_copy(tok_hbm, tok_ref, load_sem.at[0])
    wg_load = pltpu.make_async_copy(wg_hbm, wg, load_sem.at[1])
    wu_load = pltpu.make_async_copy(wu_hbm, wu, load_sem.at[2])
    wd_load = pltpu.make_async_copy(wd_hbm, wd, load_sem.at[3])
    tok_load.start()
    wg_load.start()
    wu_load.start()
    wd_load.start()
    tok_load.wait()

    tok = tok_ref[...].astype(jnp.float32)
    scale = lax.rsqrt(jnp.sum(tok * tok, axis=-1, keepdims=True) * (1.0 / D) + EPS)
    normed = (tok * scale * gain_ref[...]).astype(jnp.bfloat16)
    mine = slot(e, q, c)
    G[mine, :, :D] = normed

    pl.semaphore_wait(barrier, (E - 1) + (Q - 1) + 1)

    step = D // GATHER_CHUNKS
    spans = [
        pl.ds(j * step, step + (LANES if j == GATHER_CHUNKS - 1 else 0))
        for j in range(GATHER_CHUNKS)
    ]

    def send_experts(j):
        for d in range(1, E):
            view = G.at[mine, :, spans[j]]
            remote(view, view, az_send, az_recv.at[j, d - 1], dev(others_e[d - 1], q, c)).start()

    for j in range(GATHER_CHUNKS - 1):
        send_experts(j)

    normed_f = normed.astype(jnp.float32)
    router = router_ref[...].astype(jnp.float32)
    ids = ids_ref[...]
    first_id, second_id = ids[:, 0:1], ids[:, 1:2]
    first = jnp.zeros((B, 1), jnp.float32)
    second = jnp.zeros((B, 1), jnp.float32)
    for k in range(E):
        logit = jnp.sum(normed_f * router[k : k + 1, :], axis=-1, keepdims=True)
        first = jnp.where(first_id == k, logit, first)
        second = jnp.where(second_id == k, logit, second)
    row_at = lax.broadcasted_iota(jnp.int32, (B, 1), 0)
    alive = jnp.where(row_at < live_ref[0], 1.0, 0.0).astype(jnp.float32)
    gate0 = alive * jax.nn.sigmoid(first - second)
    gate1 = alive * jax.nn.sigmoid(second - first)
    lane = lax.broadcasted_iota(jnp.int32, (B, LANES), 1)
    low_lane = lane - E
    weight = jnp.where(first_id == lane, gate0, 0.0) + jnp.where(second_id == lane, gate1, 0.0)
    again = jnp.where(first_id == low_lane, gate0, 0.0) + jnp.where(second_id == low_lane, gate1, 0.0)
    low = again - again.astype(jnp.bfloat16).astype(jnp.float32)
    G[mine, :, pl.ds(D, LANES)] = (weight + low).astype(jnp.bfloat16)
    send_experts(GATHER_CHUNKS - 1)

    def gather_a(j):
        for d in range(E):
            s = slot(_mod(e - d, E), q, c)
            view = G.at[s, :, spans[j]]
            if d:
                remote(view, view, az_send, az_recv.at[j, d - 1], dev(e, q, c)).wait_recv()
            for dq in range(1, Q):
                remote(view, view, aq_send, aq_recv.at[j, dq - 1], dev(e, others_q[dq - 1], c)).start()
        view = G.at[pl.ds(slot(0, q, c), E), :, spans[j]]
        remote(view, view, ac_send, ac_recv.at[j, 0], dev(e, q, 1 - c)).start()

    def gather_b(j):
        for dq in range(1, Q):
            view = G.at[pl.ds(slot(0, _mod(q - dq, Q), c), E), :, spans[j]]
            wait_bytes(view, aq_recv.at[j, dq - 1])
            remote(view, view, ac_send, ac_recv.at[j, dq], dev(e, q, 1 - c)).start()

    blocks = max(1, rows // ROW_BLOCK)
    block = rows // blocks

    def over_rows(body):
        if blocks == 1:
            body(0)
        else:
            lax.fori_loop(0, blocks, lambda i, _: (body(i), 0)[1], 0)

    def lhs(i, at, width):
        view = G[pl.ds(i * (block // B), block // B), :, pl.ds(at, width)]
        return view.astype(jnp.float32).reshape(block, width)

    def gather_c(j):
        for dq in range(Q):
            view = G.at[pl.ds(slot(0, _mod(q - dq, Q), 1 - c), E), :, spans[j]]
            wait_bytes(view, ac_recv.at[j, dq])
        if j == 0:
            wg_load.wait()
            wu_load.wait()

        def body(i):
            at = pl.ds(i * block, block)
            x = lhs(i, j * step, step).astype(jnp.bfloat16)
            g = jnp.dot(x, wg[pl.ds(j * step, step), :], preferred_element_type=jnp.float32)
            u = jnp.dot(x, wu[pl.ds(j * step, step), :], preferred_element_type=jnp.float32)
            if j:
                g = g + acc_g[at, :]
                u = u + acc_u[at, :]
            if j < GATHER_CHUNKS - 1:
                acc_g[at, :] = g
                acc_u[at, :] = u
            else:
                coded = lhs(i, D, LANES)
                lanes = lax.broadcasted_iota(jnp.int32, coded.shape, 1)
                keep = (lanes == e) | (lanes == e + E)
                w = jnp.sum(jnp.where(keep, coded, 0.0), axis=-1, keepdims=True)
                hid[at, :] = (g / (1.0 + jnp.exp(-g)) * u * w).astype(jnp.bfloat16)

        over_rows(body)

    for t in range(GATHER_CHUNKS + 2):
        if t < GATHER_CHUNKS:
            gather_a(t)
        if 0 <= t - 1 < GATHER_CHUNKS:
            gather_b(t - 1)
        if 0 <= t - 2 < GATHER_CHUNKS:
            gather_c(t - 2)

    wd_load.wait()
    width = D // REDUCE_CHUNKS

    def at_rows(start, size):
        return pl.ds(pl.multiple_of(start, 16), size)

    def reduce_a(j):
        cols = pl.ds(j * width, width)

        def body(i):
            at = pl.ds(i * block, block)
            part[at, cols] = jnp.dot(
                hid[at, :], wd[:, cols], preferred_element_type=jnp.float32
            ).astype(jnp.bfloat16)

        over_rows(body)
        remote(
            part.at[at_rows((1 - c) * half, half), cols], core_in.at[:, cols],
            rc_send, rc_recv.at[j], dev(e, q, 1 - c),
        ).start()

    def reduce_b(j):
        cols = pl.ds(j * width, width)
        wait_bytes(core_in.at[:, cols], rc_recv.at[j])
        for d in list(range(1, Q)) + [0]:
            q2 = _mod(q + d, Q)
            at = at_rows(q2 * quad, quad)
            own = part[at_rows(c * half + q2 * quad, quad), cols].astype(jnp.float32)
            chip_sum[at, cols] = (own + core_in[at, cols].astype(jnp.float32)).astype(jnp.bfloat16)
            if d:
                remote(
                    chip_sum.at[at, cols], quad_in.at[d - 1, :, cols],
                    rq_send, rq_recv.at[j, d - 1], dev(e, q2, c),
                ).start()

    def reduce_c(j):
        cols = pl.ds(j * width, width)
        total = chip_sum[at_rows(q * quad, quad), cols].astype(jnp.float32)
        for d in range(1, Q):
            wait_bytes(quad_in.at[d - 1, :, cols], rq_recv.at[j, d - 1])
            total = total + quad_in[d - 1, :, cols].astype(jnp.float32)
        plane[:, :, cols] = total.reshape(E, B, width).astype(jnp.bfloat16)
        for d in range(1, E):
            remote(
                plane.at[others_e[d - 1], :, cols], plane_in.at[d - 1, :, cols],
                rz_send, rz_recv.at[j, d - 1], dev(others_e[d - 1], q, c),
            ).start()

    def reduce_d(j):
        cols = pl.ds(j * width, width)
        total = tok_ref[:, cols].astype(jnp.float32) + plane[e, :, cols].astype(jnp.float32)
        for d in range(1, E):
            wait_bytes(plane_in.at[d - 1, :, cols], rz_recv.at[j, d - 1])
            total = total + plane_in[d - 1, :, cols].astype(jnp.float32)
        out_ref[:, cols] = total.astype(jnp.bfloat16)

    for t in range(REDUCE_CHUNKS + 3):
        for lag, stage in enumerate((reduce_a, reduce_b, reduce_c, reduce_d)):
            if 0 <= t - lag < REDUCE_CHUNKS:
                stage(t - lag)

    wait_bytes(G.at[pl.ds(0, E - 1)], az_send)
    if Q > 1:
        wait_bytes(G.at[pl.ds(0, (Q - 1) * E)], aq_send)
    wait_bytes(G.at[pl.ds(0, Q * E)], ac_send)
    wait_bytes(core_in, rc_send)
    if Q > 1:
        wait_bytes(quad_in, rq_send)
    wait_bytes(plane_in, rz_send)


def local(tokens, norm_gain, router, w_gate, w_up, w_down, expert_ids, live_rows):
    devices = lax.axis_size("expert")
    B, D = tokens.shape
    E = router.shape[1]
    H = w_gate.shape[1]
    Q = devices // E // CORES
    rows = devices * B
    bf = jnp.bfloat16
    vmem = pl.BlockSpec(memory_space=pltpu.VMEM)
    anyspace = pl.BlockSpec(memory_space=pl.ANY)
    dma = pltpu.SemaphoreType.DMA
    return pl.pallas_call(
        functools.partial(kernel, E, Q, B, D, H),
        out_shape=jax.ShapeDtypeStruct((B, D), bf),
        in_specs=[
            pl.BlockSpec(memory_space=pltpu.SMEM),
            anyspace, vmem, vmem, vmem, anyspace, anyspace, anyspace,
        ],
        out_specs=vmem,
        scratch_shapes=[
            pltpu.VMEM((B, D), bf),
            pltpu.VMEM((devices, B, D + LANES), bf),
            pltpu.VMEM((D, H), bf),
            pltpu.VMEM((D, H), bf),
            pltpu.VMEM((H, D), bf),
            pltpu.VMEM((rows, H), jnp.float32),
            pltpu.VMEM((rows, H), jnp.float32),
            pltpu.VMEM((rows, H), bf),
            pltpu.VMEM((rows, D), bf),
            pltpu.VMEM((Q * E * B, D), bf),
            pltpu.VMEM((Q * E * B, D), bf),
            pltpu.VMEM((max(Q - 1, 1), E * B, D), bf),
            pltpu.VMEM((E, B, D), bf),
            pltpu.VMEM((E - 1, B, D), bf),
            dma((4,)),
            dma, dma((GATHER_CHUNKS, E - 1)),
            dma, dma((GATHER_CHUNKS, max(Q - 1, 1))),
            dma, dma((GATHER_CHUNKS, Q)),
            dma, dma((REDUCE_CHUNKS,)),
            dma, dma((REDUCE_CHUNKS, max(Q - 1, 1))),
            dma, dma((REDUCE_CHUNKS, E - 1)),
        ],
        compiler_params=pltpu.CompilerParams(
            collective_id=0, has_side_effects=True, vmem_limit_bytes=62 * 1024 * 1024
        ),
        name="routed_ffn",
    )(
        live_rows, tokens, norm_gain.reshape(1, D), router.T, expert_ids, w_gate, w_up, w_down
    )


def solution(mesh):
    return jax.shard_map(
        local,
        mesh=mesh,
        in_specs=(
            P(("groups", "expert"), None),
            P(),
            P(),
            P(None, "expert"),
            P(None, "expert"),
            P("expert", None),
            P(("groups", "expert"), None),
            P(("groups", "expert")),
        ),
        out_specs=P(("groups", "expert"), None),
        check_vma=False,
    )
```

time: 109 us -> 44.8 us (0.41)
  blocking collectives: 84.3 us -> 0 us
  Pallas kernels: 0 us -> 41 us
  matrix products: 13 us -> 0 us
  local copies, waits for them, and re-layouts: 7.44 us -> 2.89 us
  other arithmetic: 2.66 us -> 0 us
    all_to_all x2 -> x0, blocking collectives: 84.3 us -> none  [the longest x1 43.2 us: local(): lax.all_to_all(outgoing, 'expert', split_axis=0, concat_axis=0, tiled=True)]
    pallas_call x0 -> x1, Pallas kernels: none -> 41 us  [local(): pl.pallas_call(functools.partial(kernel, E, Q, B, D, H), out_shape=jax.Sh...]
    dot_general x5 -> x0, matrix products: 13 us -> none  [the longest x1 5.15 us: expert_ffn(): jnp.dot(hidden, w_down, preferred_element_type=jnp.float32)]
    reshape x3 -> x0, local copies, waits for them, and re-layouts: 5.89 us -> none  [the longest x1 2.43 us: expert_ffn(): return partial_value.reshape(count_src, count_slot, model_width)]
    reduce_sum x5 -> x0, other arithmetic: 2.52 us -> none  [the longest x1 1.2 us: local(): jnp.mean(tok_f32 * tok_f32, axis=-1, keepdims=True) + epsilon]
    unnamed x5 -> x2, local copies, waits for them, and re-layouts: 0.77 us -> 2.89 us
where the time goes in v1:
time: 44.8 us; the launch traced here: 44.6 us
  Pallas kernels  41 us (92%)
  local copies, waits for them, and re-layouts  2.89 us (6%)
  between operations  0.66 us (1%)
    pallas_call x1, Pallas kernels, local(): pl.pallas_call(functools.partial(kernel, E, Q, B, D, H), out_shape=jax.Sh...  41 us
    unnamed x2, local copies, waits for them, and re-layouts  2.89 us

profile of v1, /device:TPU:0, one launch (start us, length us, event | category | flops | bytes accessed | tf_op | source)
XLA Modules:
  0.0 44.6 jit_solution(5780010163270545597)
XLA Ops:
  0.7 1.3 %copy.9.ids_ref = s32[8,2]{1,0:T(8,128)} copy(s32[8,2]{0,1:T(2,128)} %param.14) | data formatting | bytes 128 | tf_op args[6]
  2.0 41.0 %routed_ffn.1 = bf16[8,6144]{1,0:T(8,128)(2,1)} custom-call(s32[1]{0:T(128)S(6)} %copy.11.live_ref, bf16[8,6144]{1,0:T(8,128)(2,1)} %tok_hbm.1, f32[1,6144]{1,0:T(1,128)} %bitcast.3, bf16[4,6144]{1,0:T(4,128)(2,1)} %bitcast.2, s32[8,2]{1,0:T(8,128)} %copy.9.ids_ref, bf16[6144,256]{1,0:T(8,128)(2,1)} %wg_hbm.1, bf16[6144,256]{1,0:T(8,128)(2,1)} %wu_hbm.1, ...), custom_call_target="tpu_custom_call" | custom-call | tf_op jit(solution)/shard_map/routed_ffn/pallas_call | solution.py:266
  43.1 1.5 %copy.12 = bf16[8,6144]{1,0:T(8,128)(2,1)} copy(bf16[8,6144]{1,0:T(8,128)(2,1)} %routed_ffn.1) | data formatting | bytes 196608

commit v2 on v1

--- a/solution.py
+++ b/solution.py
@@ -9,7 +9,7 @@
 
 EPS = 1e-05
 LANES = 128
-GATHER_CHUNKS = 4
+GATHER_CHUNKS = 3
 REDUCE_CHUNKS = 4
 ROW_BLOCK = 128
 CORES = 2
@@ -21,9 +21,9 @@
 
 def kernel(
     E, Q, B, D, H,
-    live_ref, tok_hbm, gain_ref, router_ref, ids_ref, wg_hbm, wu_hbm, wd_hbm,
+    live_ref, tok_hbm, gain_hbm, router_hbm, ids_hbm, wg_hbm, wu_hbm, wd_hbm,
     out_ref,
-    tok_ref, G, wg, wu, wd, acc_g, acc_u, hid, part, core_in, chip_sum, quad_in, plane, plane_in,
+    tok_ref, gain_ref, router_ref, ids_ref, G, wg, wu, wd, acc_g, acc_u, hid, part, core_in, chip_sum, quad_in, plane, plane_in,
     load_sem, az_send, az_recv, aq_send, aq_recv, ac_send, ac_recv,
     rc_send, rc_recv, rq_send, rq_recv, rz_send, rz_recv,
 ):
@@ -65,11 +65,13 @@
     wg_load = pltpu.make_async_copy(wg_hbm, wg, load_sem.at[1])
     wu_load = pltpu.make_async_copy(wu_hbm, wu, load_sem.at[2])
     wd_load = pltpu.make_async_copy(wd_hbm, wd, load_sem.at[3])
-    tok_load.start()
-    wg_load.start()
-    wu_load.start()
-    wd_load.start()
+    gain_load = pltpu.make_async_copy(gain_hbm, gain_ref, load_sem.at[4])
+    router_load = pltpu.make_async_copy(router_hbm, router_ref, load_sem.at[5])
+    ids_load = pltpu.make_async_copy(ids_hbm, ids_ref, load_sem.at[6])
+    for load in (tok_load, gain_load, router_load, ids_load, wg_load, wu_load, wd_load):
+        load.start()
     tok_load.wait()
+    gain_load.wait()
 
     tok = tok_ref[...].astype(jnp.float32)
     scale = lax.rsqrt(jnp.sum(tok * tok, axis=-1, keepdims=True) * (1.0 / D) + EPS)
@@ -89,14 +91,21 @@
         for d in range(1, E):
             view = G.at[mine, :, spans[j]]
             remote(view, view, az_send, az_recv.at[j, d - 1], dev(others_e[d - 1], q, c)).start()
+        for dq in range(1, Q):
+            view = G.at[mine, :, spans[j]]
+            remote(view, view, aq_send, aq_recv.at[j, dq - 1], dev(e, others_q[dq - 1], c)).start()
 
     for j in range(GATHER_CHUNKS - 1):
         send_experts(j)
 
     normed_f = normed.astype(jnp.float32)
+    router_load.wait()
+    ids_load.wait()
     router = router_ref[...].astype(jnp.float32)
     ids = ids_ref[...]
-    first_id, second_id = ids[:, 0:1], ids[:, 1:2]
+    diagonal = lax.broadcasted_iota(jnp.int32, (B, B), 0) == lax.broadcasted_iota(jnp.int32, (B, B), 1)
+    first_id = jnp.sum(jnp.where(diagonal, ids[0:1, :], 0), axis=-1, keepdims=True)
+    second_id = jnp.sum(jnp.where(diagonal, ids[1:2, :], 0), axis=-1, keepdims=True)
     first = jnp.zeros((B, 1), jnp.float32)
     second = jnp.zeros((B, 1), jnp.float32)
     for k in range(E):
@@ -116,11 +125,10 @@
     send_experts(GATHER_CHUNKS - 1)
 
     def gather_a(j):
-        for d in range(E):
+        for d in range(1, E):
             s = slot(_mod(e - d, E), q, c)
             view = G.at[s, :, spans[j]]
-            if d:
-                remote(view, view, az_send, az_recv.at[j, d - 1], dev(e, q, c)).wait_recv()
+            remote(view, view, az_send, az_recv.at[j, d - 1], dev(e, q, c)).wait_recv()
             for dq in range(1, Q):
                 remote(view, view, aq_send, aq_recv.at[j, dq - 1], dev(e, others_q[dq - 1], c)).start()
         view = G.at[pl.ds(slot(0, q, c), E), :, spans[j]]
@@ -237,10 +245,14 @@
             total = total + plane_in[d - 1, :, cols].astype(jnp.float32)
         out_ref[:, cols] = total.astype(jnp.bfloat16)
 
-    for t in range(REDUCE_CHUNKS + 3):
-        for lag, stage in enumerate((reduce_a, reduce_b, reduce_c, reduce_d)):
-            if 0 <= t - lag < REDUCE_CHUNKS:
-                stage(t - lag)
+    for t in range(REDUCE_CHUNKS + 1):
+        if t < REDUCE_CHUNKS:
+            reduce_a(t)
+        if t:
+            reduce_b(t - 1)
+    for stage in (reduce_c, reduce_d):
+        for t in range(REDUCE_CHUNKS):
+            stage(t)
 
     wait_bytes(G.at[pl.ds(0, E - 1)], az_send)
     if Q > 1:
@@ -268,11 +280,14 @@
         out_shape=jax.ShapeDtypeStruct((B, D), bf),
         in_specs=[
             pl.BlockSpec(memory_space=pltpu.SMEM),
-            anyspace, vmem, vmem, vmem, anyspace, anyspace, anyspace,
+            anyspace, anyspace, anyspace, anyspace, anyspace, anyspace, anyspace,
         ],
         out_specs=vmem,
         scratch_shapes=[
             pltpu.VMEM((B, D), bf),
+            pltpu.VMEM((1, D), jnp.float32),
+            pltpu.VMEM((E, D), bf),
+            pltpu.VMEM((2, B), jnp.int32),
             pltpu.VMEM((devices, B, D + LANES), bf),
             pltpu.VMEM((D, H), bf),
             pltpu.VMEM((D, H), bf),
@@ -286,7 +301,7 @@
             pltpu.VMEM((max(Q - 1, 1), E * B, D), bf),
             pltpu.VMEM((E, B, D), bf),
             pltpu.VMEM((E - 1, B, D), bf),
-            dma((4,)),
+            dma((7,)),
             dma, dma((GATHER_CHUNKS, E - 1)),
             dma, dma((GATHER_CHUNKS, max(Q - 1, 1))),
             dma, dma((GATHER_CHUNKS, Q)),
@@ -299,7 +314,7 @@
         ),
         name="routed_ffn",
     )(
-        live_rows, tokens, norm_gain.reshape(1, D), router.T, expert_ids, w_gate, w_up, w_down
+        live_rows, tokens, norm_gain.reshape(1, D), router.T, expert_ids.T, w_gate, w_up, w_down
     )
 
 

time: 44.8 us -> 38.9 us (0.87)
  Pallas kernels: 41 us -> 36.6 us
  local copies, waits for them, and re-layouts: 2.89 us -> 1.54 us
    pallas_call x1, Pallas kernels: 41 us -> 36.6 us  [local(): pl.pallas_call(functools.partial(kernel, E, Q, B, D, H), out_shape=jax.Sh...]
    unnamed x2 -> x1, local copies, waits for them, and re-layouts: 2.89 us -> 1.54 us
where the time goes in v2:
time: 38.9 us; the launch traced here: 38.8 us
  Pallas kernels  36.6 us (94%)
  local copies, waits for them, and re-layouts  1.54 us (4%)
  between operations  0.66 us (2%)
    pallas_call x1, Pallas kernels, local(): pl.pallas_call(functools.partial(kernel, E, Q, B, D, H), out_shape=jax.Sh...  36.6 us
    unnamed x1, local copies, waits for them, and re-layouts  1.54 us

profile of v2, /device:TPU:0, one launch (start us, length us, event | category | flops | bytes accessed | tf_op | source)
XLA Modules:
  0.0 38.8 jit_solution(7787111602890410383)
XLA Ops:
  0.7 36.6 %routed_ffn.1 = bf16[8,6144]{1,0:T(8,128)(2,1)} custom-call(s32[1]{0:T(128)S(6)} %copy.10.live_ref, bf16[8,6144]{1,0:T(8,128)(2,1)} %tok_hbm.1, f32[1,6144]{1,0:T(1,128)} %bitcast.4, bf16[4,6144]{1,0:T(4,128)(2,1)} %bitcast.3, s32[2,8]{1,0:T(2,128)} %bitcast.5, bf16[6144,256]{1,0:T(8,128)(2,1)} %wg_hbm.1, bf16[6144,256]{1,0:T(8,128)(2,1)} %wu_hbm.1, ...), custom_call_target="tpu_custom_call" | custom-call | tf_op jit(solution)/shard_map/routed_ffn/pallas_call | solution.py:278
  37.2 1.5 %copy.11 = bf16[8,6144]{1,0:T(8,128)(2,1)} copy(bf16[8,6144]{1,0:T(8,128)(2,1)} %routed_ffn.1) | data formatting | bytes 196608

commit v3 on v2

--- a/solution.py
+++ b/solution.py
@@ -10,7 +10,7 @@
 EPS = 1e-05
 LANES = 128
 GATHER_CHUNKS = 3
-REDUCE_CHUNKS = 4
+REDUCE_CHUNKS = 6
 ROW_BLOCK = 128
 CORES = 2
 
@@ -79,7 +79,6 @@
     mine = slot(e, q, c)
     G[mine, :, :D] = normed
 
-    pl.semaphore_wait(barrier, (E - 1) + (Q - 1) + 1)
 
     step = D // GATHER_CHUNKS
     spans = [
@@ -95,8 +94,6 @@
             view = G.at[mine, :, spans[j]]
             remote(view, view, aq_send, aq_recv.at[j, dq - 1], dev(e, others_q[dq - 1], c)).start()
 
-    for j in range(GATHER_CHUNKS - 1):
-        send_experts(j)
 
     normed_f = normed.astype(jnp.float32)
     router_load.wait()
@@ -122,7 +119,9 @@
     again = jnp.where(first_id == low_lane, gate0, 0.0) + jnp.where(second_id == low_lane, gate1, 0.0)
     low = again - again.astype(jnp.bfloat16).astype(jnp.float32)
     G[mine, :, pl.ds(D, LANES)] = (weight + low).astype(jnp.bfloat16)
-    send_experts(GATHER_CHUNKS - 1)
+    pl.semaphore_wait(barrier, (E - 1) + (Q - 1) + 1)
+    for j in range(GATHER_CHUNKS):
+        send_experts(j)
 
     def gather_a(j):
         for d in range(1, E):

time: 38.9 us -> 38.6 us (level)
  no operation moved by 1% of the time
where the time goes in v3:
time: 38.6 us; the launch traced here: 38.5 us
  Pallas kernels  36.3 us (94%)
  local copies, waits for them, and re-layouts  1.54 us (4%)
  between operations  0.66 us (2%)
    pallas_call x1, Pallas kernels, local(): pl.pallas_call(functools.partial(kernel, E, Q, B, D, H), out_shape=jax.Sh...  36.3 us
    unnamed x1, local copies, waits for them, and re-layouts  1.54 us

profile of v3, /device:TPU:0, one launch (start us, length us, event | category | flops | bytes accessed | tf_op | source)
XLA Modules:
  0.0 38.5 jit_solution(5201381618295173925)
XLA Ops:
  0.7 36.3 %routed_ffn.1 = bf16[8,6144]{1,0:T(8,128)(2,1)} custom-call(s32[1]{0:T(128)S(6)} %copy.10.live_ref, bf16[8,6144]{1,0:T(8,128)(2,1)} %tok_hbm.1, f32[1,6144]{1,0:T(1,128)} %bitcast.4, bf16[4,6144]{1,0:T(4,128)(2,1)} %bitcast.3, s32[2,8]{1,0:T(2,128)} %bitcast.5, bf16[6144,256]{1,0:T(8,128)(2,1)} %wg_hbm.1, bf16[6144,256]{1,0:T(8,128)(2,1)} %wu_hbm.1, ...), custom_call_target="tpu_custom_call" | custom-call | tf_op jit(solution)/shard_map/routed_ffn/pallas_call | solution.py:277
  37.0 1.5 %copy.11 = bf16[8,6144]{1,0:T(8,128)(2,1)} copy(bf16[8,6144]{1,0:T(8,128)(2,1)} %routed_ffn.1) | data formatting | bytes 196608
